TPU v7x, 256 devices: a whole 4x4x8 slice. The times are simulated.
256 devices in a mesh: users: 64 (over x, z, y_hi), items: 4 (over y_lo, core).
Axes of the slice: x: 4, y: 4 (y_hi: 2, y_lo: 2; y = y_hi * 2 + y_lo), z: 8, core: 2. Of those that a mesh axis runs over, the one named last changes fastest.
Arguments:
- user_factors: bfloat16 [131072, 128], P('users'), may hold values from -0.5 to 0.5
- item_factors: float32 [4, 4, 512, 128], P('items', None, 'users'), may hold values from -6 to 6
- tile_user: int32 [64, 4, 4, 16], P('users', 'items'), may hold values from 0 to 7, as said below
- tile_item: int32 [64, 4, 4, 16], P('users', 'items'), may hold values from 0 to 1, as said below
- tile_count: int32 [64, 4, 4], P('users', 'items'), may hold values from 1 to 16, as said below
- ratings: bfloat16 [64, 4, 4, 16, 256, 256], P('users', 'items'), may hold values from -6 to 6
- mask: int32 [64, 4, 4, 16, 32, 256], P('users', 'items'), may hold values from 0 to 255
Outputs:
- new_items: float32 [4, 4, 512, 128], P('items', None, 'users')
- user_grad: float32 [131072, 128], P(('users', 'items'))
Inputs may be any that keep to these rules, and one draw needn't show every extreme that they name: `tile_user`: index of a user tile within its user block. `tile_item`: index of an item tile within its panel; the pairs (tile_user, tile_item) of one user block, owner and panel are distinct. Only the first tile_count slots of a user block, owner and panel hold observed tiles; the other slots are to be ignored. For every owner and panel some user block fills all 16 slots. Bit k of word mask[..., w, j] marks the rating in row 8 * w + k, column j of the tile as observed.
All inputs are finite; a program needn't handle non-finite values.
Results may differ from a plain program's by a relative error of at most 0.0031.
Values may be sent and summed in bfloat16 or wider, within the bound.
A program may use at most 128 MiB of HBM per device.

v0:
```python
import math
import jax
import jax.numpy as jnp
from jax import lax
from jax.sharding import PartitionSpec as P


def shards(user_factors, item_factors, tile_user, tile_item, tile_count, ratings, mask):
    users_count = lax.axis_size("users")
    rank_width = user_factors.shape[1]
    tile_side = ratings.shape[-1]
    user_tiles = user_factors.shape[0] // tile_side
    step_count = item_factors.shape[1]
    slot_count = ratings.shape[3]
    local_rows = item_factors.shape[2]
    panel_rows = local_rows * users_count
    panel_tiles = panel_rows // tile_side
    user_blocks = user_factors.reshape(user_tiles, tile_side, rank_width)
    step_rate = 8.0 / math.sqrt(tile_side * users_count)
    shifts = jnp.arange(8, dtype=jnp.int32)
    user_sum = jnp.zeros((user_tiles, tile_side, rank_width), jnp.float32)
    updated = []
    for step_index in range(step_count):
        panel_bf = lax.all_gather(
            item_factors[0, step_index].astype(jnp.bfloat16), "users", axis=0, tiled=True
        )
        tiles_of_panel = panel_bf.reshape(panel_tiles, tile_side, rank_width)
        user_index = tile_user[0, 0, step_index]
        item_index = tile_item[0, 0, step_index]
        user_rows = user_blocks[user_index]
        item_rows = tiles_of_panel[item_index]
        predicted = jnp.einsum(
            "tir,tjr->tij", user_rows, item_rows, preferred_element_type=jnp.float32
        )
        mask_bits = mask[0, 0, step_index][:, :, None, :] >> shifts[None, None, :, None] & 1
        observed = mask_bits.reshape(slot_count, tile_side, tile_side).astype(jnp.float32)
        live_slots = (jnp.arange(slot_count) < tile_count[0, 0, step_index]).astype(jnp.float32)
        errors = (
            observed
            * live_slots[:, None, None]
            * (predicted - ratings[0, 0, step_index].astype(jnp.float32))
        ).astype(jnp.bfloat16)
        tile_grad = jnp.einsum(
            "tij,tir->tjr", errors, user_rows, preferred_element_type=jnp.float32
        )
        item_onehot = (
            item_index[:, None] == jnp.arange(panel_tiles, dtype=jnp.int32)[None, :]
        ).astype(jnp.float32)
        panel_grad = jnp.einsum(
            "tp,tjr->pjr", item_onehot, tile_grad, precision=lax.Precision.HIGHEST
        ).reshape(panel_rows, rank_width)
        user_part = jnp.einsum(
            "tij,tjr->tir", errors, item_rows, preferred_element_type=jnp.float32
        )
        user_onehot = (
            user_index[:, None] == jnp.arange(user_tiles, dtype=jnp.int32)[None, :]
        ).astype(jnp.float32)
        user_sum = user_sum + jnp.einsum(
            "tu,tir->uir", user_onehot, user_part, precision=lax.Precision.HIGHEST
        )
        whole_sum = lax.psum(panel_grad, "users")
        own_rows = lax.dynamic_slice_in_dim(
            whole_sum, lax.axis_index("users") * local_rows, local_rows, 0
        )
        updated.append(0.95 * item_factors[0, step_index] - step_rate * own_rows)
    new_items = jnp.stack(updated)[None]
    user_terms = user_sum.reshape(user_tiles * tile_side, rank_width) / 32.0
    user_grad = lax.psum_scatter(user_terms, "items", scatter_dimension=0, tiled=True)
    return (new_items, user_grad)


def solution(mesh):
    return jax.shard_map(
        shards,
        mesh=mesh,
        in_specs=(
            P("users", None),
            P("items", None, "users", None),
            P("users", "items", None, None),
            P("users", "items", None, None),
            P("users", "items", None),
            P("users", "items", None, None, None, None),
            P("users", "items", None, None, None, None),
        ),
        out_specs=(P("items", None, "users", None), P(("users", "items"), None)),
        check_vma=False,
    )
```

profile of v0, /device:TPU:8, one launch (start us, length us, event | category | flops | bytes accessed | tf_op | source)
XLA Modules:
  0.0 1480.3 jit_solution(12672225782933500393)
XLA Ops:
  8.1 1.5 fusion.89
  9.5 1.2 compare_convert_fusion.3
  10.7 1.2 compare_convert_fusion.2
  11.9 1.1 compare_convert_fusion
  13.0 1.3 compare_convert_fusion.1
  14.3 1.4 slice_bitcast_fusion.11
  15.7 0.8 fusion.76
  16.6 0.7 fusion.88
  18.0 184.3 %all-gather = bf16[1,1,512,128]{3,2,1,0:T(8,128)(2,1)S(1)} all-gather(bf16[1,1,8,128]{3,2,1,0:T(8,128)(2,1)S(1)} %get-tuple-element.14), channel_id=2, replica_groups=mesh['users'=64,'items'=4] {'users'}, dimensions={2}, use_global_device_ids=true | all-gather | bytes 133120 | tf_op jit(solution)/shard_map/all_gather | solution.py:24
  202.4 174.5 %all-gather.1 = bf16[1,1,512,128]{3,2,1,0:T(8,128)(2,1)S(1)} all-gather(bf16[1,1,8,128]{3,2,1,0:T(8,128)(2,1)S(1)} %get-tuple-element.15), channel_id=3, replica_groups=mesh['users'=64,'items'=4] {'users'}, dimensions={2}, use_global_device_ids=true | all-gather | bytes 133120 | tf_op jit(solution)/shard_map/all_gather | solution.py:24
  376.9 178.1 %all-gather.2 = bf16[1,1,512,128]{3,2,1,0:T(8,128)(2,1)S(1)} all-gather(bf16[1,1,8,128]{3,2,1,0:T(8,128)(2,1)S(1)} %get-tuple-element.16), channel_id=4, replica_groups=mesh['users'=64,'items'=4] {'users'}, dimensions={2}, use_global_device_ids=true | all-gather | bytes 133120 | tf_op jit(solution)/shard_map/all_gather | solution.py:24
  555.0 174.5 %all-gather.3 = bf16[1,1,512,128]{3,2,1,0:T(8,128)(2,1)S(1)} all-gather(bf16[1,1,8,128]{3,2,1,0:T(8,128)(2,1)S(1)} %get-tuple-element.17), channel_id=5, replica_groups=mesh['users'=64,'items'=4] {'users'}, dimensions={2}, use_global_device_ids=true | all-gather | bytes 133120 | tf_op jit(solution)/shard_map/all_gather | solution.py:24
  729.5 1.7 gather_fusion.4
  731.2 1.7 gather_fusion.6
  732.8 1.7 gather_fusion.2
  734.5 1.6 gather_fusion
  736.2 2.7 slice_bitcast_fusion.3
  738.9 1.6 gather_fusion.1
  740.5 3.5 fusion.7
  744.1 0.8 fusion.90
  744.9 2.0 fusion.34
  746.8 0.7 copy.9
  747.6 1.8 gather_fusion.3
  749.3 3.5 fusion.5
  752.9 0.8 fusion.91
  754.2 2.0 fusion.32
  756.2 0.7 copy.10
  757.0 1.7 gather_fusion.7
  758.7 3.5 fusion.1
  762.3 0.8 fusion.93
  763.5 2.1 fusion.28
  765.7 0.7 copy.12
  766.4 1.7 gather_fusion.5
  768.1 3.4 fusion.3
  771.6 0.8 fusion.92
  772.9 2.0 fusion.30
  774.9 0.7 copy.11
  775.7 2.7 fusion.95
  778.5 0.7 fusion.97
  779.2 0.9 copy-done.5
  781.1 2.0 fusion.24
  783.1 2.0 fusion.20
  785.0 2.0 fusion.22
  787.0 0.7 fusion.94
  787.8 2.2 fusion.45
  790.0 1.2 copy.13
  791.2 680.4 %all-reduce.3.cloned.1.call-done = (f32[512,128]{1,0:T(8,128)}, f32[512,128]{1,0:T(8,128)}, f32[512,128]{1,0:T(8,128)}, f32[512,128]{1,0:T(8,128)}) async-done(((f32[512,128]{1,0:T(8,128)}, f32[512,128]{1,0:T(8,128)}, f32[512,128]{1,0:T(8,128)}, f32[512,128]{1,0:T(8,128)}), (f32[512,128]{1,0:T(8,128)}, f32[512,128]{1,0:T(8,128)}, f32[512,128]{1,0:T(8,128)}, ...) | async-done | bytes 1048592 | tf_op jit(solution)/shard_map/psum | solution.py:61
  1471.5 0.7 fusion.51
  (59 shorter events, 4.2 us)
Async XLA Ops:
  8.0 721.5 %copy-start = (bf16[2048,128]{1,0:T(8,128)(2,1)S(1)}, bf16[2048,128]{1,0:T(8,128)(2,1)}, u32[]{:S(2)}) copy-start(bf16[2048,128]{1,0:T(8,128)(2,1)} %param.7) | copy-start | bytes 1572868
  8.0 1463.5 %all-reduce.3.cloned.1.call-start = ((), (), s32[]{:S(2)}) async-start(), calls=%async_computation.2 | async-start | bytes 2097152 | tf_op jit(solution)/shard_map/psum | solution.py:61
  740.5 3.6 copy-start.12
  744.1 0.8 copy-start.17
  749.3 3.5 copy-start.11
  752.9 1.4 copy-start.1
  752.9 1.3 copy-start.16
  754.2 4.4 copy-start.18
  754.2 4.4 copy-start.20
  758.7 3.5 copy-start.9
  762.2 1.3 copy-start.2
  762.2 1.3 copy-start.15
  763.5 4.5 copy-start.19
  768.1 3.5 copy-start.7
  771.5 1.4 copy-start.4
  772.9 2.8 copy-start.14
  775.6 697.2 %reduce-scatter.2.cloned.1.call-start = ((), (), s32[]{:S(2)}) async-start(), calls=%async_computation.1 | async-start | bytes 1310720 | tf_op jit(solution)/shard_map/reduce_scatter | solution.py:68
  775.7 2.7 copy-start.3
  775.7 2.8 copy-start.8
  778.5 1.6 copy-start.5
  778.5 1.9 copy-start.10
  785.0 2.0 copy-start.6
  790.0 681.6 %copy-start.13 = (f32[1,4,8,128]{3,2,1,0:T(8,128)S(1)}, f32[1,4,8,128]{3,2,1,0:T(8,128)}, u32[]{:S(2)}) copy-start(f32[1,4,8,128]{3,2,1,0:T(8,128)} %param.8) | copy-start | bytes 49156
Sparse Core Ops, SparseCore 0:
  775.8 695.7 all-reduce.2
Sparse Core Ops, SparseCore 1:
  791.3 17.1 reduce-scatter.1
where the time goes:
time: 1480 us
  blocking collectives  711 us (48%)
  waiting for transfers between devices  680 us (46%)
  matrix products  38.1 us (3%)
  local copies, waits for them, and re-layouts  27.5 us (2%)
  between operations  15.9 us (1%)
    all_gather x4, blocking collectives, shards(): lax.all_gather(item_factors[0, step_index].astype(jnp.bfloat16), 'users',...  711 us
    psum x1, waiting for transfers between devices, shards(): whole_sum = lax.psum(panel_grad, 'users')  680 us
  transfers between devices with their start and end apart: 2, of which 1 were waited for; matrix products, arithmetic and copies ran while one was open for 1% of the time, Pallas kernels for 0%

commit v1 on v0

--- a/solution.py
+++ b/solution.py
@@ -3,6 +3,7 @@
 import jax.numpy as jnp
 from jax import lax
 from jax.sharding import PartitionSpec as P
+from jax.lax import all_to_all, axis_size
 
 
 def shards(user_factors, item_factors, tile_user, tile_item, tile_count, ratings, mask):
@@ -21,8 +22,16 @@
     user_sum = jnp.zeros((user_tiles, tile_side, rank_width), jnp.float32)
     updated = []
     for step_index in range(step_count):
-        panel_bf = lax.all_gather(
-            item_factors[0, step_index].astype(jnp.bfloat16), "users", axis=0, tiled=True
+        panel_bf = jnp.concatenate(
+            all_to_all(
+                jnp.stack(
+                    axis_size("users") * [item_factors[0, step_index].astype(jnp.bfloat16)], axis=0
+                ),
+                axis_name="users",
+                split_axis=0,
+                concat_axis=0,
+            ),
+            axis=0,
         )
         tiles_of_panel = panel_bf.reshape(panel_tiles, tile_side, rank_width)
         user_index = tile_user[0, 0, step_index]

time: 1480 us -> 838 us (0.57)
  blocking collectives: 711 us -> 0 us
  starting transfers between devices: 0.08 us -> 43.6 us
  waiting for transfers between devices: 680 us -> 703 us
    all_gather x4 -> x0, blocking collectives: 711 us -> none  [shards(): lax.all_gather(item_factors[0, step_index].astype(jnp.bfloat16), 'users',...]
    all_to_all x0 -> x4, starting transfers between devices: none -> 43.4 us  [shards(): all_to_all(jnp.stack(axis_size('users') * [item_factors[0, step_index].as...]
  transfers between devices with their start and end apart: 2 -> 6, of which waited for: 1 -> 4; matrix products, arithmetic and copies ran while one was open for 1% -> 6% of each run, Pallas kernels for 0% -> 0%
where the time goes in v1:
time: 838 us; the launch traced here: 837 us
  waiting for transfers between devices  703 us (84%)
  starting transfers between devices  43.6 us (5%)
  matrix products  43.2 us (5%)
  local copies, waits for them, and re-layouts  26.4 us (3%)
  between operations  15.9 us (2%)
    psum x1, waiting for transfers between devices, shards(): whole_sum = lax.psum(panel_grad, 'users')  692 us
    all_to_all x4, starting transfers between devices, shards(): all_to_all(jnp.stack(axis_size('users') * [item_factors[0, step_index].as...  43.4 us
  transfers between devices with their start and end apart: 6, of which 4 were waited for; matrix products, arithmetic and copies ran while one was open for 6% of the time, Pallas kernels for 0%

profile of v1, /device:TPU:8, one launch (start us, length us, event | category | flops | bytes accessed | tf_op | source)
XLA Modules:
  0.0 837.0 jit_solution(11438922863057177773)
XLA Ops:
  8.0 0.8 fusion.60
  9.5 13.7 %all-to-all-start.1 = ((bf16[64,8,128]{2,1,0:T(8,128)(2,1)}), bf16[64,8,128]{2,1,0:T(8,128)(2,1)S(1)}, u32[]{:S(2)}, u32[]{:S(2)}) async-start(bf16[64,8,128]{2,1,0:T(8,128)(2,1)} %stack.20), calls=%async_computation.1 | async-start | bytes 262144 | tf_op jit(solution)/shard_map/all_to_all | solution.py:26
  23.2 0.8 slice_bitcast_fusion.10
  24.0 0.8 slice_bitcast_fusion.11
  24.8 0.8 fusion.80
  25.7 1.5 fusion.92
  29.9 1.6 gather_fusion.4
  31.6 1.7 gather_fusion.6
  33.3 0.7 gather_fusion.2
  34.1 1.8 gather_fusion
  35.8 2.8 slice_bitcast_fusion.3
  39.3 12.7 %all-to-all-start.3 = ((bf16[64,8,128]{2,1,0:T(8,128)(2,1)}), bf16[64,8,128]{2,1,0:T(8,128)(2,1)S(1)}, u32[]{:S(2)}, u32[]{:S(2)}) async-start(bf16[64,8,128]{2,1,0:T(8,128)(2,1)} %stack.24), calls=%async_computation.3 | async-start | bytes 262144 | tf_op jit(solution)/shard_map/all_to_all | solution.py:26
  52.0 0.7 gather_fusion.3
  52.8 2.8 fusion.5
  55.6 2.0 fusion.98
  57.6 0.8 fusion.94
  58.4 5.8 all-to-all-done.3
  64.9 7.0 all-to-all-start.2
  71.8 1.7 gather_fusion.7
  73.5 3.5 fusion.1
  77.1 2.0 fusion.100
  79.1 2.1 fusion.96
  81.3 2.7 all-to-all-done.2
  84.7 10.0 %all-to-all-start = ((bf16[64,8,128]{2,1,0:T(8,128)(2,1)}), bf16[64,8,128]{2,1,0:T(8,128)(2,1)S(1)}, u32[]{:S(2)}, u32[]{:S(2)}) async-start(bf16[64,8,128]{2,1,0:T(8,128)(2,1)} %stack.18), calls=%async_computation | async-start | bytes 262144 | tf_op jit(solution)/shard_map/all_to_all | solution.py:26
  94.9 1.7 gather_fusion.5
  96.6 3.5 fusion.3
  100.2 2.1 fusion.99
  102.3 2.1 fusion.95
  104.4 2.5 all-to-all-done
  106.9 1.7 gather_fusion.1
  108.6 3.4 fusion.7
  112.1 0.8 fusion.93
  113.4 2.0 fusion.34
  115.4 0.7 copy.9
  116.1 2.0 fusion.32
  118.1 0.7 copy.10
  118.8 2.0 fusion.28
  120.8 0.7 copy.12
  121.6 2.2 fusion.30
  123.8 0.7 copy.11
  124.5 3.0 fusion.24
  127.6 2.0 fusion.20
  129.6 2.0 fusion.22
  131.6 0.7 fusion.97
  132.9 2.2 fusion.45
  135.1 1.2 copy.13
  136.3 691.9 %all-reduce.3.cloned.1.call-done = (f32[512,128]{1,0:T(8,128)}, f32[512,128]{1,0:T(8,128)}, f32[512,128]{1,0:T(8,128)}, f32[512,128]{1,0:T(8,128)}) async-done(((f32[512,128]{1,0:T(8,128)}, f32[512,128]{1,0:T(8,128)}, f32[512,128]{1,0:T(8,128)}, f32[512,128]{1,0:T(8,128)}), (f32[512,128]{1,0:T(8,128)}, f32[512,128]{1,0:T(8,128)}, f32[512,128]{1,0:T(8,128)}, ...) | async-done | bytes 1048592 | tf_op jit(solution)/shard_map/psum | solution.py:70
  828.2 0.7 fusion.51
  (61 shorter events, 7.5 us)
Async XLA Ops:
  8.0 21.9 %copy-start = (bf16[2048,128]{1,0:T(8,128)(2,1)S(1)}, bf16[2048,128]{1,0:T(8,128)(2,1)}, u32[]{:S(2)}) copy-start(bf16[2048,128]{1,0:T(8,128)(2,1)} %param.7) | copy-start | bytes 1572868
  9.5 29.1 %all-to-all-start.1 = ((bf16[64,8,128]{2,1,0:T(8,128)(2,1)}), bf16[64,8,128]{2,1,0:T(8,128)(2,1)S(1)}, u32[]{:S(2)}, u32[]{:S(2)}) async-start(bf16[64,8,128]{2,1,0:T(8,128)(2,1)} %stack.20), calls=%async_computation.1 | async-start | bytes 262144 | tf_op jit(solution)/shard_map/all_to_all | solution.py:26
  34.1 18.7 %copy-start.12 = (bf16[16,256,128]{2,1,0:T(8,128)(2,1)}, bf16[16,256,128]{2,1,0:T(8,128)(2,1)S(1)}, u32[]{:S(2)}) copy-start(bf16[16,256,128]{2,1,0:T(8,128)(2,1)S(1)} %gather_fusion.2) | copy-start | bytes 3145732
  39.3 24.9 %all-to-all-start.3 = ((bf16[64,8,128]{2,1,0:T(8,128)(2,1)}), bf16[64,8,128]{2,1,0:T(8,128)(2,1)S(1)}, u32[]{:S(2)}, u32[]{:S(2)}) async-start(bf16[64,8,128]{2,1,0:T(8,128)(2,1)} %stack.24), calls=%async_computation.3 | async-start | bytes 262144 | tf_op jit(solution)/shard_map/all_to_all | solution.py:26
  55.6 2.0 copy-start.13
  64.9 19.1 %all-to-all-start.2 = ((bf16[64,8,128]{2,1,0:T(8,128)(2,1)}), bf16[64,8,128]{2,1,0:T(8,128)(2,1)S(1)}, u32[]{:S(2)}, u32[]{:S(2)}) async-start(bf16[64,8,128]{2,1,0:T(8,128)(2,1)} %stack.22), calls=%async_computation.2 | async-start | bytes 262144 | tf_op jit(solution)/shard_map/all_to_all | solution.py:26
  73.5 3.5 copy-start.14
  77.1 2.1 copy-start.11
  84.7 22.2 %all-to-all-start = ((bf16[64,8,128]{2,1,0:T(8,128)(2,1)}), bf16[64,8,128]{2,1,0:T(8,128)(2,1)S(1)}, u32[]{:S(2)}, u32[]{:S(2)}) async-start(bf16[64,8,128]{2,1,0:T(8,128)(2,1)} %stack.18), calls=%async_computation | async-start | bytes 262144 | tf_op jit(solution)/shard_map/all_to_all | solution.py:26
  94.7 733.5 %all-reduce.3.cloned.1.call-start = ((), (), s32[]{:S(2)}) async-start(), calls=%async_computation.6 | async-start | bytes 2097152 | tf_op jit(solution)/shard_map/psum | solution.py:70
  96.6 3.5 copy-start.15
  100.2 2.1 copy-start.9
  108.6 3.5 copy-start.8
  112.0 1.4 copy-start.6
  115.4 3.4 copy-start.1
  118.1 3.5 copy-start.2
  120.8 3.7 copy-start.3
  124.5 3.1 copy-start.4
  127.5 702.0 %reduce-scatter.2.cloned.1.call-start = ((), (), s32[]{:S(2)}) async-start(), calls=%async_computation.5 | async-start | bytes 1310720 | tf_op jit(solution)/shard_map/reduce_scatter | solution.py:77
  127.6 2.0 copy-start.5
  129.6 2.0 copy-start.7
  129.6 2.0 copy-start.10
  131.6 1.2 copy-start.16
  135.1 693.1 %copy-start.17 = (f32[1,4,8,128]{3,2,1,0:T(8,128)S(1)}, f32[1,4,8,128]{3,2,1,0:T(8,128)}, u32[]{:S(2)}) copy-start(f32[1,4,8,128]{3,2,1,0:T(8,128)} %param.8) | copy-start | bytes 49156
Sparse Core Ops, SparseCore 0:
  127.7 700.4 all-reduce.2
Sparse Core Ops, SparseCore 1:
  136.3 21.4 reduce-scatter.1
